TPU v7x, 32 devices: a whole 2x2x4 slice. The times are simulated.
32 devices in a mesh: wide: 8 (over z, x), narrow: 4 (over y, core).
Axes of the slice: x: 2, y: 2, z: 4, core: 2. Of those that a mesh axis runs over, the one named last changes fastest.
Arguments:
- fine_in: bfloat16 [16, 16, 64, 512], P(None, None, 'wide', 'narrow'), may hold values from -6 to 6
- coarse_in: bfloat16 [64, 16, 16, 128], P(None, 'wide', 'narrow'), may hold values from -6 to 6
- w_fine1: bfloat16 [16, 16, 3, 3, 3], replicated, may hold values from -0.3125 to 0.3125
- b_fine1: float32 [16], replicated, may hold values from -3 to 3
- w_fine2: bfloat16 [16, 16, 3, 3, 3], replicated, may hold values from -0.3125 to 0.3125
- b_fine2: float32 [16], replicated, may hold values from -3 to 3
- w_coarse1: bfloat16 [64, 80, 3, 3, 3], replicated, may hold values from -0.125 to 0.125
- b_coarse1: float32 [64], replicated, may hold values from -3 to 3
- w_coarse2: bfloat16 [64, 64, 3, 3, 3], replicated, may hold values from -0.15625 to 0.15625
- b_coarse2: float32 [64], replicated, may hold values from -3 to 3
- w_proj: bfloat16 [16, 64], replicated, may hold values from -0.75 to 0.75
Outputs:
- fine_out: bfloat16 [16, 16, 64, 512], P(None, None, 'wide', 'narrow')
- coarse_out: bfloat16 [64, 16, 16, 128], P(None, 'wide', 'narrow')
All inputs are finite; a program needn't handle non-finite values.
Results may differ from a plain program's by a relative error of at most 0.0075.
Values may be sent and summed in bfloat16 or wider, within the bound.
A program may use at most 192 MiB of HBM per device.

v0:
```python
import jax
import jax.numpy as jnp
from jax import lax
from jax.sharding import PartitionSpec as P


def padded_2(array, sides, width):
    for axis, dim in sides:
        count, length = (lax.axis_size(axis), array.shape[dim])
        up = [(i, (i + 1) % count) for i in range(count - 1)]
        down = [(j, i) for i, j in up]
        last = lax.slice_in_dim(array, length - width, length, axis=dim)
        initial = lax.slice_in_dim(array, 0, width, axis=dim)
        before = lax.ppermute(last, axis, up)
        after = lax.ppermute(initial, axis, down)
        array = jnp.concatenate([before, array, after], axis=dim)
    return array


def convolve(field, kernel, offset, margins):
    result = lax.conv_general_dilated(
        field[None],
        kernel,
        (1, 1, 1),
        margins,
        dimension_numbers=("NCDHW", "OIDHW", "NCDHW"),
        preferred_element_type=jnp.float32,
    )[0]
    return result + offset[:, None, None, None]


def project(features, w_proj):
    return jnp.einsum("fc,czyx->fzyx", w_proj, features, preferred_element_type=jnp.float32).astype(
        jnp.bfloat16
    )


def local(
    fine_in,
    coarse_in,
    w_fine1,
    b_fine1,
    w_fine2,
    b_fine2,
    w_coarse1,
    b_coarse1,
    w_coarse2,
    b_coarse2,
    w_proj,
):
    fine_margins = ((1, 1), (0, 0), (0, 0))
    coarse_margins = ((0, 0), (0, 0), (1, 1))
    edged = padded_2(fine_in, (("wide", 2), ("narrow", 3)), 1)
    hidden = jnp.maximum(convolve(edged, w_fine1, b_fine1, fine_margins), 0.0).astype(jnp.bfloat16)
    channels, depth, rows_y, rows_x = hidden.shape
    pooled = (
        hidden.astype(jnp.float32)
        .reshape(channels, depth, rows_y // 4, 4, rows_x // 4, 4)
        .mean(axis=(3, 5))
        .astype(jnp.bfloat16)
    )
    arrived = lax.all_to_all(
        lax.all_to_all(pooled, "wide", split_axis=1, concat_axis=2, tiled=True),
        "narrow",
        split_axis=2,
        concat_axis=3,
        tiled=True,
    )
    stacked = jnp.concatenate([coarse_in, arrived], axis=0)
    padded = padded_2(stacked, (("wide", 1), ("narrow", 2)), 1)
    coarse_mid = jnp.maximum(convolve(padded, w_coarse1, b_coarse1, coarse_margins), 0.0).astype(
        jnp.bfloat16
    )
    mid_padded = padded_2(coarse_mid, (("wide", 1), ("narrow", 2)), 1)
    coarse_out = jnp.maximum(
        convolve(mid_padded, w_coarse2, b_coarse2, coarse_margins), 0.0
    ).astype(jnp.bfloat16)
    edged_mid = padded_2(hidden, (("wide", 2), ("narrow", 3)), 1)
    fine_term = convolve(edged_mid, w_fine2, b_fine2, fine_margins)
    context = project(coarse_out, w_proj)
    partway = lax.all_to_all(context, "narrow", split_axis=3, concat_axis=2, tiled=True)
    context = lax.all_to_all(partway, "wide", split_axis=2, concat_axis=1, tiled=True)
    small_y = context.shape[2]
    small_x = context.shape[3]
    widened = jnp.broadcast_to(
        context[:, :, :, None, :, None], (channels, depth, small_y, 4, small_x, 4)
    ).reshape(channels, depth, rows_y, rows_x)
    fine_out = (fine_term + widened.astype(jnp.float32)).astype(jnp.bfloat16)
    return (fine_out, coarse_out)


def solution(mesh):
    return jax.shard_map(
        local,
        mesh=mesh,
        in_specs=(
            P(None, None, "wide", "narrow"),
            P(None, "wide", "narrow", None),
            P(),
            P(),
            P(),
            P(),
            P(),
            P(),
            P(),
            P(),
            P(),
        ),
        out_specs=(P(None, None, "wide", "narrow"), P(None, "wide", "narrow", None)),
        check_vma=False,
    )
```

profile of v0, /device:TPU:1, one launch (start us, length us, event | category | flops | bytes accessed | tf_op | source)
XLA Modules:
  0.0 269.3 jit_solution(15416653241995295753)
XLA Ops:
  4.3 4.6 %collective-permute-start = (bf16[16,16,1,128]{1,0,3,2:T(8,128)(2,1)S(1)}, bf16[16,16,1,128]{1,0,3,2:T(8,128)(2,1)S(1)}, u32[]{:S(2)}, u32[]{:S(2)}) collective-permute-start(bf16[16,16,1,128]{1,0,3,2:T(8,128)(2,1)S(1)} %copy.241), channel_id=1, source_target_pairs={{0,4},{4,8},{8,12},{12,16},{16,20},{20,24},{24,28},{1,5},{5,9},{9,... | collective-permute-start | bytes 196616 | tf_op jit(solution)/shard_map/ppermute | solution.py:14
  8.9 4.9 %copy.243 = bf16[16,16,8,128]{1,0,3,2:T(8,128)(2,1)} copy(bf16[16,16,8,128]{3,2,1,0:T(8,128)(2,1)} %param.11) | data formatting | bytes 1048576 | tf_op args[0]
  13.8 4.3 %collective-permute-done.1 = bf16[16,16,1,128]{1,0,3,2:T(8,128)(2,1)S(1)} collective-permute-done((bf16[16,16,1,128]{1,0,3,2:T(8,128)(2,1)S(1)}, bf16[16,16,1,128]{1,0,3,2:T(8,128)(2,1)S(1)}, u32[]{:S(2)}, u32[]{:S(2)}) %collective-permute-start.1) | collective-permute-done | bytes 65568 | tf_op jit(solution)/shard_map/ppermute | solution.py:15
  18.1 12.1 %collective-permute-done = bf16[16,16,1,128]{1,0,3,2:T(8,128)(2,1)S(1)} collective-permute-done((bf16[16,16,1,128]{1,0,3,2:T(8,128)(2,1)S(1)}, bf16[16,16,1,128]{1,0,3,2:T(8,128)(2,1)S(1)}, u32[]{:S(2)}, u32[]{:S(2)}) %collective-permute-start) | collective-permute-done | bytes 65568 | tf_op jit(solution)/shard_map/ppermute | solution.py:14
  42.2 4.9 %copy.245 = bf16[16,16,10,128]{3,1,2,0:T(8,128)(2,1)S(1)} copy(bf16[16,16,10,128]{1,0,3,2:T(8,128)(2,1)} %copy-done.2) | data formatting | bytes 1310720 | tf_op jit(solution)/shard_map/concatenate | solution.py:16
  50.2 5.3 %reshape.20 = bf16[16,16,10,1,8,17]{5,4,1,2,0,3:T(8,128)(2,1)} reshape(bf16[16,16,10,1,136]{4,1,2,0,3:T(8,128)(2,1)S(1)} %pad) | data formatting | bytes 1392640 | tf_op jit(solution)/shard_map/conv_general_dilated | solution.py:21
  55.5 12.2 %copy.248 = bf16[16,16,10,1,8,17]{0,4,5,2,1,3:T(8,128)(2,1)} copy(bf16[16,16,10,1,8,17]{5,4,1,2,0,3:T(8,128)(2,1)} %reshape.20) | data formatting | bytes 1392640 | tf_op jit(solution)/shard_map/conv_general_dilated | solution.py:21
  69.0 14.8 %broadcast_select_fusion.1 = f32[16,8,8,17,16]{4,2,3,1,0:T(8,128)} fusion(pred[8,17]{0,1:T(8,128)(4,1)S(1)} %copy-done.11, bf16[16,16,3,3,3]{1,0,4,3,2:T(8,128)(2,1)S(1)} %copy-done.9, bf16[16,16,10,1,7,2]{0,4,5,2,1,3:T(8,128)(2,1)S(1)} %slice.74, bf16[16,16,10,1,8,17]{0,4,5,2,1,3:T(8,128)(2,1)} %copy.248), kind=kOutput, calls=%fused_computation.19 | convolution fusion | flops 233234432 | bytes 1896072 | tf_op jit(solution)/shard_map/conv_general_dilated | solution.py:21
  83.8 11.4 %copy.249 = f32[16,8,8,17,16]{3,2,4,1,0:T(8,128)} copy(f32[16,8,8,17,16]{4,2,3,1,0:T(8,128)} %broadcast_select_fusion.1) | data formatting | bytes 2228224 | tf_op jit(solution)/shard_map/conv_general_dilated | solution.py:21
  95.2 5.8 %reshape.24 = f32[16,8,1,136,16]{3,4,1,0,2:T(8,128)S(1)} reshape(f32[16,8,8,17,16]{3,2,4,1,0:T(8,128)} %copy.249) | data formatting | bytes 2228224 | tf_op jit(solution)/shard_map/conv_general_dilated | solution.py:21
  102.1 6.6 %copy.258 = f32[1,16,16,8,128]{2,1,4,3,0:T(8,128)} copy(f32[1,16,16,8,128]{4,1,3,2,0:T(8,128)} %slice_bitcast_fusion.1) | data formatting | bytes 2097152 | tf_op jit(solution)/shard_map/conv_general_dilated | solution.py:21
  108.7 4.7 %convert_reduce_fusion = f32[16,16,2,32]{1,0,3,2:T(8,128)S(1)} fusion(f32[16,16,2,4,32,4]{1,0,5,4,3,2:T(8,128)} %bitcast.126, f32[16]{0:T(128)S(1)} %copy-done.5), kind=kLoop, calls=%fused_computation.3 | loop fusion | flops 1294336 | bytes 1114176 | tf_op jit(solution)/shard_map/reduce_sum | solution.py:59
  113.8 11.3 %all_to_all.63 = bf16[8,2,1024]{2,1,0:T(2,128)(2,1)S(1)} all-to-all(bf16[8,2,1024]{2,1,0:T(2,128)(2,1)S(1)} %reshape.71), channel_id=1, replica_groups=mesh['wide'=8,'narrow'=4] {'wide'}, dimensions={0} | all-to-all | bytes 65536 | tf_op jit(solution)/shard_map/all_to_all | solution.py:63
  146.8 3.8 %collective-permute-start.4 = (bf16[16,16,1,128]{3,0,2,1:T(8,128)(2,1)S(1)}, bf16[16,16,1,128]{3,0,2,1:T(8,128)(2,1)S(1)}, u32[]{:S(2)}, u32[]{:S(2)}) collective-permute-start(bf16[16,16,1,128]{3,0,2,1:T(8,128)(2,1)S(1)} %get-tuple-element.20), channel_id=1, source_target_pairs={{0,4},{4,8},{8,12},{12,16},{16,20},{20,24},{24,28},{1,5},{5,9},{9,... | collective-permute-start | bytes 196616 | tf_op jit(solution)/shard_map/ppermute | solution.py:14
  156.4 4.0 %collective-permute-start.12 = (bf16[64,1,4,128]{0,2,3,1:T(4,128)(2,1)S(1)}, bf16[64,1,4,128]{0,2,3,1:T(4,128)(2,1)S(1)}, u32[]{:S(2)}, u32[]{:S(2)}) collective-permute-start(bf16[64,1,4,128]{0,2,3,1:T(4,128)(2,1)S(1)} %get-tuple-element.28), channel_id=1, source_target_pairs={{0,4},{4,8},{8,12},{12,16},{16,20},{20,24},{24,28},{1,5},{5,9},{9,... | collective-permute-start | bytes 196616 | tf_op jit(solution)/shard_map/ppermute | solution.py:14
  163.5 3.8 %collective-permute-done.13 = bf16[64,1,4,128]{0,2,3,1:T(4,128)(2,1)S(1)} collective-permute-done((bf16[64,1,4,128]{0,2,3,1:T(4,128)(2,1)S(1)}, bf16[64,1,4,128]{0,2,3,1:T(4,128)(2,1)S(1)}, u32[]{:S(2)}, u32[]{:S(2)}) %collective-permute-start.13) | collective-permute-done | bytes 65568 | tf_op jit(solution)/shard_map/ppermute | solution.py:15
  169.0 4.4 %collective-permute-start.14 = (bf16[64,4,1,128]{0,2,3,1:T(2,128)(2,1)}, bf16[64,4,1,128]{0,2,3,1:T(2,128)(2,1)}, u32[]{:S(2)}, u32[]{:S(2)}) collective-permute-start(bf16[64,4,1,128]{0,2,3,1:T(2,128)(2,1)} %get-tuple-element.22), channel_id=1, source_target_pairs={{0,1},{1,2},{2,3},{4,5},{5,6},{6,7},{8,9},{9,10},{10,11},{12,13},{... | collective-permute-start | bytes 196616 | tf_op jit(solution)/shard_map/ppermute | solution.py:14
  199.8 5.3 %reshape.70 = bf16[16,16,10,1,8,17]{5,4,0,2,1,3:T(8,128)(2,1)} reshape(bf16[16,16,10,1,136]{4,0,2,1,3:T(8,128)(2,1)S(1)} %pad.2) | data formatting | bytes 1392640 | tf_op jit(solution)/shard_map/conv_general_dilated | solution.py:21
  205.1 11.4 %copy.256 = bf16[16,16,10,1,8,17]{0,4,5,2,1,3:T(8,128)(2,1)} copy(bf16[16,16,10,1,8,17]{5,4,0,2,1,3:T(8,128)(2,1)} %reshape.70) | data formatting | bytes 1392640 | tf_op jit(solution)/shard_map/conv_general_dilated | solution.py:21
  222.6 14.8 %broadcast_select_fusion = f32[16,8,8,17,16]{4,2,3,1,0:T(8,128)} fusion(pred[8,17]{0,1:T(8,128)(4,1)S(1)} %copy-done.11, bf16[16,16,3,3,3]{1,0,4,3,2:T(8,128)(2,1)S(1)} %copy-done.10, bf16[16,16,10,1,7,2]{0,4,5,2,1,3:T(8,128)(2,1)S(1)} %slice.80, bf16[16,16,10,1,8,17]{0,4,5,2,1,3:T(8,128)(2,1)} %copy.256), kind=kOutput, calls=%fused_computation.18 | convolution fusion | flops 233234432 | bytes 1896072 | tf_op jit(solution)/shard_map/conv_general_dilated | solution.py:21
  237.3 11.4 %copy.257 = f32[16,8,8,17,16]{3,2,4,1,0:T(8,128)} copy(f32[16,8,8,17,16]{4,2,3,1,0:T(8,128)} %broadcast_select_fusion) | data formatting | bytes 2228224 | tf_op jit(solution)/shard_map/conv_general_dilated | solution.py:21
  248.7 5.8 %reshape.31 = f32[16,8,1,136,16]{3,4,1,0,2:T(8,128)S(1)} reshape(f32[16,8,8,17,16]{3,2,4,1,0:T(8,128)} %copy.257) | data formatting | bytes 2228224 | tf_op jit(solution)/shard_map/conv_general_dilated | solution.py:21
  255.9 4.0 %broadcast_in_dim.26 = f32[16,16,2,4,32,4]{1,0,5,4,3,2:T(8,128)} broadcast(f32[16,16,2,32]{1,0,3,2:T(8,128)S(1)} %copy.284), dimensions={0,1,2,4} | broadcast | bytes 1114112 | tf_op jit(solution)/shard_map/broadcast_in_dim | solution.py:85
  259.9 6.7 %copy.285 = f32[16,16,8,128]{3,0,2,1:T(8,128)} copy(f32[16,16,8,128]{1,0,3,2:T(8,128)} %bitcast.127) | data formatting | bytes 2097152 | tf_op jit(solution)/shard_map/convert_element_type | solution.py:88
  (129 shorter events, 89.5 us)
Async XLA Ops:
  0.6 153.3 %copy-start = (bf16[64,80,3,3,3]{1,0,4,3,2:T(8,128)(2,1)S(1)}, bf16[64,80,3,3,3]{1,0,4,3,2:T(8,128)(2,1)}, u32[]{:S(2)}) copy-start(bf16[64,80,3,3,3]{1,0,4,3,2:T(8,128)(2,1)} %param.17) | copy-start | bytes 829444
  2.6 15.6 %collective-permute-start.1 = (bf16[16,16,1,128]{1,0,3,2:T(8,128)(2,1)S(1)}, bf16[16,16,1,128]{1,0,3,2:T(8,128)(2,1)S(1)}, u32[]{:S(2)}, u32[]{:S(2)}) collective-permute-start(bf16[16,16,1,128]{1,0,3,2:T(8,128)(2,1)S(1)} %copy.242), channel_id=1, source_target_pairs={{4,0},{8,4},{12,8},{16,12},{20,16},{24,20},{28,24},{5,1},{9,5},{13... | collective-permute-start | bytes 196616 | tf_op jit(solution)/shard_map/ppermute | solution.py:15
  4.3 26.0 %collective-permute-start = (bf16[16,16,1,128]{1,0,3,2:T(8,128)(2,1)S(1)}, bf16[16,16,1,128]{1,0,3,2:T(8,128)(2,1)S(1)}, u32[]{:S(2)}, u32[]{:S(2)}) collective-permute-start(bf16[16,16,1,128]{1,0,3,2:T(8,128)(2,1)S(1)} %copy.241), channel_id=1, source_target_pairs={{0,4},{4,8},{8,12},{12,16},{16,20},{20,24},{24,28},{1,5},{5,9},{9,... | collective-permute-start | bytes 196616 | tf_op jit(solution)/shard_map/ppermute | solution.py:14
  36.2 10.9 %collective-permute-start.3 = (bf16[16,16,10,1]{1,0,3,2:T(8,128)(2,1)S(1)}, bf16[16,16,10,1]{1,0,3,2:T(8,128)(2,1)S(1)}, u32[]{:S(2)}, u32[]{:S(2)}) collective-permute-start(bf16[16,16,10,1]{1,0,3,2:T(8,128)(2,1)S(1)} %get-tuple-element.17), channel_id=1, source_target_pairs={{1,0},{2,1},{3,2},{5,4},{6,5},{7,6},{9,8},{10,9},{11,10},{13,12},{... | collective-permute-start | bytes 15368 | tf_op jit(solution)/shard_map/ppermute | solution.py:15
  38.6 9.6 %collective-permute-start.2 = (bf16[16,16,10,1]{1,0,3,2:T(8,128)(2,1)S(1)}, bf16[16,16,10,1]{1,0,3,2:T(8,128)(2,1)S(1)}, u32[]{:S(2)}, u32[]{:S(2)}) collective-permute-start(bf16[16,16,10,1]{1,0,3,2:T(8,128)(2,1)S(1)} %get-tuple-element.16), channel_id=1, source_target_pairs={{0,1},{1,2},{2,3},{4,5},{5,6},{6,7},{8,9},{9,10},{10,11},{12,13},{... | collective-permute-start | bytes 15368 | tf_op jit(solution)/shard_map/ppermute | solution.py:14
  55.5 13.5 %copy-start.9 = (bf16[16,16,3,3,3]{1,0,4,3,2:T(8,128)(2,1)S(1)}, bf16[16,16,3,3,3]{1,0,4,3,2:T(8,128)(2,1)}, u32[]{:S(2)}) copy-start(bf16[16,16,3,3,3]{1,0,4,3,2:T(8,128)(2,1)} %param.13) | copy-start | bytes 41476
  55.5 13.5 %copy-start.11 = (pred[8,17]{0,1:T(8,128)(4,1)S(1)}, pred[8,17]{0,1:T(8,128)(4,1)}, u32[]{:S(2)}) copy-start(pred[8,17]{0,1:T(8,128)(4,1)} %constant.24) | copy-start | bytes 412
  108.7 21.1 %copy-start.3 = (bf16[64,2,4,128]{3,2,1,0:T(4,128)(2,1)S(1)}, bf16[64,2,4,128]{3,2,1,0:T(4,128)(2,1)}, u32[]{:S(2)}) copy-start(bf16[64,2,4,128]{3,2,1,0:T(4,128)(2,1)} %param.12) | copy-start | bytes 393220
  126.1 6.8 %all-to-all-start.1 = ((bf16[4,2,2048]{2,1,0:T(2,128)(2,1)}), bf16[4,2,2048]{2,1,0:T(2,128)(2,1)S(1)}, u32[]{:S(2)}, u32[]{:S(2)}) async-start(bf16[4,2,2048]{2,1,0:T(2,128)(2,1)} %reshape.73), calls=%async_computation.1 | async-start | bytes 65536 | tf_op jit(solution)/shard_map/all_to_all | solution.py:62
  133.4 3.5 %collective-permute-start.8 = (bf16[80,1,4,128]{3,2,1,0:T(4,128)(2,1)S(1)}, bf16[80,1,4,128]{3,2,1,0:T(4,128)(2,1)S(1)}, u32[]{:S(2)}, u32[]{:S(2)}) collective-permute-start(bf16[80,1,4,128]{3,2,1,0:T(4,128)(2,1)S(1)} %get-tuple-element.30), channel_id=1, source_target_pairs={{0,4},{4,8},{8,12},{12,16},{16,20},{20,24},{24,28},{1,5},{5,9},{9,... | collective-permute-start | bytes 245768 | tf_op jit(solution)/shard_map/ppermute | solution.py:14
  135.4 5.2 %collective-permute-start.9 = (bf16[80,1,4,128]{3,2,1,0:T(4,128)(2,1)S(1)}, bf16[80,1,4,128]{3,2,1,0:T(4,128)(2,1)S(1)}, u32[]{:S(2)}, u32[]{:S(2)}) collective-permute-start(bf16[80,1,4,128]{3,2,1,0:T(4,128)(2,1)S(1)} %get-tuple-element.31), channel_id=1, source_target_pairs={{4,0},{8,4},{12,8},{16,12},{20,16},{24,20},{28,24},{5,1},{9,5},{13... | collective-permute-start | bytes 245768 | tf_op jit(solution)/shard_map/ppermute | solution.py:15
  141.1 10.8 %collective-permute-start.10 = (bf16[80,4,1,128]{3,2,1,0:T(2,128)(2,1)S(1)}, bf16[80,4,1,128]{3,2,1,0:T(2,128)(2,1)S(1)}, u32[]{:S(2)}, u32[]{:S(2)}) collective-permute-start(bf16[80,4,1,128]{3,2,1,0:T(2,128)(2,1)S(1)} %get-tuple-element.26), channel_id=1, source_target_pairs={{0,1},{1,2},{2,3},{4,5},{5,6},{6,7},{8,9},{9,10},{10,11},{12,13},{... | collective-permute-start | bytes 245768 | tf_op jit(solution)/shard_map/ppermute | solution.py:14
  144.9 7.1 %collective-permute-start.11 = (bf16[80,4,1,128]{3,2,1,0:T(2,128)(2,1)S(1)}, bf16[80,4,1,128]{3,2,1,0:T(2,128)(2,1)S(1)}, u32[]{:S(2)}, u32[]{:S(2)}) collective-permute-start(bf16[80,4,1,128]{3,2,1,0:T(2,128)(2,1)S(1)} %get-tuple-element.27), channel_id=1, source_target_pairs={{1,0},{2,1},{3,2},{5,4},{6,5},{7,6},{9,8},{10,9},{11,10},{13,12},{... | collective-permute-start | bytes 245768 | tf_op jit(solution)/shard_map/ppermute | solution.py:15
  146.8 14.9 %collective-permute-start.4 = (bf16[16,16,1,128]{3,0,2,1:T(8,128)(2,1)S(1)}, bf16[16,16,1,128]{3,0,2,1:T(8,128)(2,1)S(1)}, u32[]{:S(2)}, u32[]{:S(2)}) collective-permute-start(bf16[16,16,1,128]{3,0,2,1:T(8,128)(2,1)S(1)} %get-tuple-element.20), channel_id=1, source_target_pairs={{0,4},{4,8},{8,12},{12,16},{16,20},{20,24},{24,28},{1,5},{5,9},{9,... | collective-permute-start | bytes 196616 | tf_op jit(solution)/shard_map/ppermute | solution.py:14
  150.6 11.1 %collective-permute-start.5 = (bf16[16,16,1,128]{3,0,2,1:T(8,128)(2,1)S(1)}, bf16[16,16,1,128]{3,0,2,1:T(8,128)(2,1)S(1)}, u32[]{:S(2)}, u32[]{:S(2)}) collective-permute-start(bf16[16,16,1,128]{3,0,2,1:T(8,128)(2,1)S(1)} %get-tuple-element.21), channel_id=1, source_target_pairs={{4,0},{8,4},{12,8},{16,12},{20,16},{24,20},{28,24},{5,1},{9,5},{13... | collective-permute-start | bytes 196616 | tf_op jit(solution)/shard_map/ppermute | solution.py:15
  156.4 7.1 %collective-permute-start.12 = (bf16[64,1,4,128]{0,2,3,1:T(4,128)(2,1)S(1)}, bf16[64,1,4,128]{0,2,3,1:T(4,128)(2,1)S(1)}, u32[]{:S(2)}, u32[]{:S(2)}) collective-permute-start(bf16[64,1,4,128]{0,2,3,1:T(4,128)(2,1)S(1)} %get-tuple-element.28), channel_id=1, source_target_pairs={{0,4},{4,8},{8,12},{12,16},{16,20},{20,24},{24,28},{1,5},{5,9},{9,... | collective-permute-start | bytes 196616 | tf_op jit(solution)/shard_map/ppermute | solution.py:14
  160.4 7.0 %collective-permute-start.13 = (bf16[64,1,4,128]{0,2,3,1:T(4,128)(2,1)S(1)}, bf16[64,1,4,128]{0,2,3,1:T(4,128)(2,1)S(1)}, u32[]{:S(2)}, u32[]{:S(2)}) collective-permute-start(bf16[64,1,4,128]{0,2,3,1:T(4,128)(2,1)S(1)} %get-tuple-element.29), channel_id=1, source_target_pairs={{4,0},{8,4},{12,8},{16,12},{20,16},{24,20},{28,24},{5,1},{9,5},{13... | collective-permute-start | bytes 196616 | tf_op jit(solution)/shard_map/ppermute | solution.py:15
  169.0 19.3 %collective-permute-start.14 = (bf16[64,4,1,128]{0,2,3,1:T(2,128)(2,1)}, bf16[64,4,1,128]{0,2,3,1:T(2,128)(2,1)}, u32[]{:S(2)}, u32[]{:S(2)}) collective-permute-start(bf16[64,4,1,128]{0,2,3,1:T(2,128)(2,1)} %get-tuple-element.22), channel_id=1, source_target_pairs={{0,1},{1,2},{2,3},{4,5},{5,6},{6,7},{8,9},{9,10},{10,11},{12,13},{... | collective-permute-start | bytes 196616 | tf_op jit(solution)/shard_map/ppermute | solution.py:14
  173.4 16.0 %collective-permute-start.15 = (bf16[64,4,1,128]{0,2,3,1:T(2,128)(2,1)}, bf16[64,4,1,128]{0,2,3,1:T(2,128)(2,1)S(1)}, u32[]{:S(2)}, u32[]{:S(2)}) collective-permute-start(bf16[64,4,1,128]{0,2,3,1:T(2,128)(2,1)} %get-tuple-element.23), channel_id=1, source_target_pairs={{1,0},{2,1},{3,2},{5,4},{6,5},{7,6},{9,8},{10,9},{11,10},{13,12},{... | collective-permute-start | bytes 196616 | tf_op jit(solution)/shard_map/ppermute | solution.py:15
  176.7 6.9 %collective-permute-start.6 = (bf16[16,16,10,1]{1,0,3,2:T(8,128)(2,1)S(1)}, bf16[16,16,10,1]{1,0,3,2:T(8,128)(2,1)S(1)}, u32[]{:S(2)}, u32[]{:S(2)}) collective-permute-start(bf16[16,16,10,1]{1,0,3,2:T(8,128)(2,1)S(1)} %copy.250), channel_id=1, source_target_pairs={{0,1},{1,2},{2,3},{4,5},{5,6},{6,7},{8,9},{9,10},{10,11},{12,13},{... | collective-permute-start | bytes 15368 | tf_op jit(solution)/shard_map/ppermute | solution.py:14
  181.4 5.3 %collective-permute-start.7 = (bf16[16,16,10,1]{1,0,3,2:T(8,128)(2,1)S(1)}, bf16[16,16,10,1]{1,0,3,2:T(8,128)(2,1)S(1)}, u32[]{:S(2)}, u32[]{:S(2)}) collective-permute-start(bf16[16,16,10,1]{1,0,3,2:T(8,128)(2,1)S(1)} %copy.251), channel_id=1, source_target_pairs={{1,0},{2,1},{3,2},{5,4},{6,5},{7,6},{9,8},{10,9},{11,10},{13,12},{... | collective-permute-start | bytes 15368 | tf_op jit(solution)/shard_map/ppermute | solution.py:15
  195.5 22.3 %all-to-all-start.2 = ((bf16[4,2,2048]{2,1,0:T(2,128)(2,1)}), bf16[4,2,2048]{2,1,0:T(2,128)(2,1)S(1)}, u32[]{:S(2)}, u32[]{:S(2)}) async-start(bf16[4,2,2048]{2,1,0:T(2,128)(2,1)} %reshape.75), calls=%async_computation.2 | async-start | bytes 65536 | tf_op jit(solution)/shard_map/all_to_all | solution.py:81
  205.1 17.5 %copy-start.10 = (bf16[16,16,3,3,3]{1,0,4,3,2:T(8,128)(2,1)S(1)}, bf16[16,16,3,3,3]{1,0,4,3,2:T(8,128)(2,1)}, u32[]{:S(2)}) copy-start(bf16[16,16,3,3,3]{1,0,4,3,2:T(8,128)(2,1)} %param.15) | copy-start | bytes 41476
  218.9 36.4 %all-to-all-start.3 = ((bf16[8,2,1024]{2,1,0:T(2,128)(2,1)}), bf16[8,2,1024]{2,1,0:T(2,128)(2,1)S(1)}, u32[]{:S(2)}, u32[]{:S(2)}) async-start(bf16[8,2,1024]{2,1,0:T(2,128)(2,1)} %reshape.77), calls=%async_computation.3 | async-start | bytes 65536 | tf_op jit(solution)/shard_map/all_to_all | solution.py:82
  (7 other events, 33.9 us)
where the time goes:
time: 274 us; the launch traced here: 269 us
  local copies, waits for them, and re-layouts  124 us (45%)
  starting transfers between devices  53.9 us (20%)
  matrix products  34.9 us (13%)
  waiting for transfers between devices  30.7 us (11%)
  other arithmetic  13.2 us (5%)
  blocking collectives  11.3 us (4%)
    conv_general_dilated x18, local copies, waits for them, and re-layouts, convolve(): lax.conv_general_dilated(field[None], kernel, (1, 1, 1), margins, dimensi...  79.3 us
    conv_general_dilated x4, matrix products, convolve(): lax.conv_general_dilated(field[None], kernel, (1, 1, 1), margins, dimensi...  34.7 us
    ppermute x8, starting transfers between devices, padded_2(): before = lax.ppermute(last, axis, up)  29.9 us
    ppermute x8, waiting for transfers between devices, padded_2(): before = lax.ppermute(last, axis, up)  13.9 us
    ppermute x8, waiting for transfers between devices, padded_2(): after = lax.ppermute(initial, axis, down)  13.7 us
    unnamed x38, local copies, waits for them, and re-layouts  13.6 us
    ppermute x8, starting transfers between devices, padded_2(): after = lax.ppermute(initial, axis, down)  13.5 us
    all_to_all x1, blocking collectives, local(): lax.all_to_all(pooled, 'wide', split_axis=1, concat_axis=2, tiled=True)  11.3 us
  transfers between devices with their start and end apart: 19, of which 7 were waited for; matrix products, arithmetic and copies ran while one was open for 27% of the time, Pallas kernels for 0%

commit v1 on v0

v1 whole, which is shorter than its diff:
```python
import functools

import jax
import jax.numpy as jnp
from jax import lax
from jax.experimental import pallas as pl
from jax.experimental.pallas import tpu as pltpu
from jax.sharding import PartitionSpec as P

F32, BF16 = jnp.float32, jnp.bfloat16


def dot(a, b):
    return jnp.dot(a, b, preferred_element_type=F32)


def lanes(shape):
    return lax.broadcasted_iota(jnp.int32, shape, len(shape) - 1)


def kernel(
    dims,
    fine, coarse, k1, k2, kc, kp, km, b1, b2, bc1, bc2, wp,
    out, cout,
    halo1, edge1, side1, halo2, edge2, side2, band, x3, hidden,
    cbuf, pool, prcv, xc3, xp3, wc, wq, x3m, wm, ctx, crcv,
    fsend, frecv, hsend, hrecv, csend, crecv, psend, precv, tsend, trecv, lsem,
):
    nw, nn, depth, cf, cc, fy, cz, cy, cx, xs = dims
    rows, crow = depth * cf, cz * cc
    reach = cy // 2
    w, n = lax.axis_index("wide"), lax.axis_index("narrow")

    def at(a, b):
        return {"wide": a, "narrow": b}

    barrier = pltpu.get_barrier_semaphore()

    def greet(i, carry):
        a, b = i // nn, i % nn

        @pl.when(jnp.logical_or(a != w, b != n))
        def _():
            pl.semaphore_signal(barrier, inc=1, device_id=at(a, b))

        return carry

    lax.fori_loop(0, nw * nn, greet, 0)

    def remote(src, dst, ssem, rsem, a, b):
        return pltpu.make_async_remote_copy(
            src_ref=src, dst_ref=dst, send_sem=ssem, recv_sem=rsem,
            device_id=at(a, b), device_id_type=pl.DeviceIdType.MESH)

    def inside(a, b):
        ok_a = jnp.logical_and(a >= 0, a < nw)
        ok_b = jnp.logical_and(b >= 0, b < nn)
        return jnp.logical_and(ok_a, ok_b)

    lane = lanes((rows, cx))

    def pack(row_of, edge):
        total = jnp.zeros((rows, cx), F32)
        for y in range(fy):
            row = row_of(y).astype(F32)
            first = pltpu.roll(row, y, 1) if y else row
            total = jnp.where(lane == y, first, total)
            total = jnp.where(lane == 64 + y, pltpu.roll(row, 65 + y, 1), total)
        edge[...] = total.astype(BF16)

    around = ((-1, 0), (1, 0), (0, -1), (0, 1), (-1, -1), (-1, 1), (1, -1), (1, 1))

    def fine_copies(top, bottom, edge, halo, side, ssem, rsem):
        made = []
        for i, (da, db) in enumerate(around):
            if i == 0:
                src, dst = bottom, halo.at[0]
            elif i == 1:
                src, dst = top, halo.at[1]
            else:
                src, dst = edge, side.at[i - 2]
            made.append((dst, w - da, n - db, w + da, n + db,
                         remote(src, dst, ssem.at[i], rsem.at[i], w - da, n - db)))
        return made

    def send(made):
        for dst, a, b, _, _, copy in made:
            pl.when(inside(a, b))(copy.start)

    def clear(made):
        for dst, _, _, a, b, copy in made:
            @pl.when(jnp.logical_not(inside(a, b)))
            def _(dst=dst):
                dst[...] = jnp.zeros(dst.shape, BF16)

    def receive(made):
        for dst, _, _, a, b, copy in made:
            pl.when(inside(a, b))(copy.wait_recv)

    def sent(made):
        for dst, a, b, _, _, copy in made:
            pl.when(inside(a, b))(copy.wait_send)

    def expand(row_of, halo, side):
        left, right, ul, ur, dl, dr = [side[i].astype(F32) for i in range(6)]
        for y in range(-1, fy + 1):
            if y < 0:
                raw, lcol, rcol, j = halo[0], ul, ur, fy - 1
            elif y == fy:
                raw, lcol, rcol, j = halo[1], dl, dr, 0
            else:
                raw, lcol, rcol, j = row_of(y), left, right, y
            row = raw.astype(F32)
            cols = pl.ds((y + 1) * cx, cx)
            x3[pl.ds(rows, rows), cols] = raw
            x3[pl.ds(0, rows), cols] = jnp.where(
                lane == 0, pltpu.roll(lcol, 64 - j, 1), pltpu.roll(row, 1, 1)).astype(BF16)
            moved = pltpu.roll(rcol, cx - 1 - j, 1)
            x3[pl.ds(2 * rows, rows), cols] = jnp.where(
                lane == cx - 1, moved, pltpu.roll(row, cx - 1, 1)).astype(BF16)

    def bands(base):
        spot = lanes((cf, rows))
        for tap in range(9):
            dy, dx = tap // 3, tap % 3
            piece = base[tap]
            for z in range(depth):
                part = pltpu.roll(piece, z * cf, 1) if z else piece
                if z == 0:
                    part = jnp.where(spot >= rows - cf, 0.0, part)
                if z == depth - 1:
                    part = jnp.where(spot < cf, 0.0, part)
                band[dy, pl.ds(z * cf, cf), pl.ds(dx * rows, rows)] = part.astype(BF16)

    def short_bands(base, target, count, step):
        size, width = base.shape[1], base.shape[2]
        for tap in range(9):
            dy, dx = tap // 3, tap % 3
            piece = base[tap]
            for z in range(count):
                part = pltpu.roll(piece, z * step, 1) if z else piece
                target[dy, pl.ds(z * size, size), pl.ds(dx * width, width)] = part.astype(BF16)

    def conv(weights, field, start, width):
        total = None
        for dy in range(3):
            term = dot(weights[dy], field[:, pl.ds(start + dy * cx, width)])
            total = term if total is None else total + term
        return total

    pack(lambda y: fine[y], edge1)
    first = fine_copies(fine.at[0], fine.at[fy - 1], edge1, halo1, side1, fsend, frecv)
    cmade = []
    for i, (da, db) in enumerate(around):
        zpos = pl.ds((da + 1) * crow, crow)
        if db == 0:
            src, dst = coarse, cbuf.at[pl.ds(2, cy), zpos]
        elif db < 0:
            src, dst = coarse.at[pl.ds(cy - 2, 2)], cbuf.at[pl.ds(0, 2), zpos]
        else:
            src, dst = coarse.at[pl.ds(0, 2)], cbuf.at[pl.ds(cy + 2, 2), zpos]
        cmade.append((dst, w - da, n - db, w + da, n + db,
                      remote(src, dst, csend.at[i], crecv.at[i], w - da, n - db)))
    pl.semaphore_wait(barrier, nw * nn - 1)
    send(first)
    send(cmade)
    clear(first)
    clear(cmade)
    cbuf[pl.ds(2, cy), pl.ds(crow, crow), :] = coarse[...]
    pool[pl.ds(0, 2 * cf), :] = jnp.zeros((2 * cf, cx), BF16)
    pool[pl.ds(2 * cf + rows, 2 * cf), :] = jnp.zeros((2 * cf, cx), BF16)
    bands(k1)
    receive(first)
    expand(lambda y: fine[y], halo1, side1)

    source = lax.broadcasted_iota(jnp.int32, (cx, cx), 0)
    target = lanes((cx, cx))
    for g in range(fy // 4):
        place = jnp.where(target == source // 4 + g * xs, 1.0, 0.0).astype(BF16)
        total = None
        for h in range(2):
            y = g * 4 + h * 2
            both = jnp.maximum(conv(band, x3, y * cx, 2 * cx) + b1[...], 0.0).astype(BF16)
            for k in range(2):
                row = both[:, k * cx:(k + 1) * cx]
                hidden[y + k] = row
                term = dot(row, place)
                total = term if total is None else total + term
        if g == 0:
            summed = total
        else:
            summed = summed + total
    pool[pl.ds(2 * cf, rows), :] = (summed * (1.0 / 16.0)).astype(BF16)

    tall = (cz + 4) * cf

    def pooled_copy(a, which, b):
        k = w - b * reach + 1
        return remote(pool.at[pl.ds(pl.multiple_of(a * cz * cf, cf), tall)], prcv.at[k, n],
                      psend.at[which, a], precv.at[k, n], a, b)

    def local_copy():
        k = w - n * reach + 1
        return pltpu.make_async_copy(pool.at[pl.ds(pl.multiple_of(w * cz * cf, cf), tall)],
                                     prcv.at[k, n], precv.at[k, n])

    home = w // reach
    rest = w % reach
    targets = (
        (home, None),
        (home - 1, jnp.logical_and(rest == 0, home >= 1)),
        (home + 1, jnp.logical_and(rest == reach - 1, home + 1 < nn)),
    )

    def each_target(start):
        for which, (b, ok) in enumerate(targets):
            def step(a, carry, which=which, b=b, ok=ok):
                self_ = jnp.logical_and(a == w, b == n)
                go = jnp.logical_not(self_)
                if ok is not None:
                    go = jnp.logical_and(go, ok)

                @pl.when(go)
                def _():
                    copy = pooled_copy(a, which, b)
                    if start:
                        copy.start()
                    else:
                        copy.wait_send()

                if start:
                    mine = self_ if ok is None else jnp.logical_and(self_, ok)

                    @pl.when(mine)
                    def _():
                        local_copy().start()

                return carry

            lax.fori_loop(0, nw, step, 0)

    each_target(True)
    pack(lambda y: hidden[y], edge2)
    second = fine_copies(hidden.at[0], hidden.at[fy - 1], edge2, halo2, side2, hsend, hrecv)
    send(second)
    clear(second)

    short_bands(kc, wc, cz + 2, cc)
    short_bands(kp, wq, cz + 2, cf)
    short_bands(km, wm, cz, cc)
    receive(cmade)

    def spread(field, raw, y, height):
        row = raw.astype(F32)
        spot = lanes(row.shape)
        cols = pl.ds(y * cx, cx)
        field[pl.ds(height, raw.shape[0]), cols] = raw
        field[pl.ds(0, raw.shape[0]), cols] = jnp.where(
            spot == 0, 0.0, pltpu.roll(row, 1, 1)).astype(BF16)
        field[pl.ds(2 * height, raw.shape[0]), cols] = jnp.where(
            spot == cx - 1, 0.0, pltpu.roll(row, cx - 1, 1)).astype(BF16)

    for y in range(cy + 4):
        spread(xc3, cbuf[y], y, (cz + 4) * cc)
    high = wq.shape[2] // 3
    if high > tall:
        for dx in range(3):
            xp3[pl.ds(dx * high + tall, high - tall), :] = jnp.zeros(
                (high - tall, xp3.shape[1]), BF16)
    lowl = lax.broadcasted_iota(jnp.int32, (cx, 2 * cx), 0)
    wide_ = lanes((cx, 2 * cx))
    for k in range(reach + 2):
        tile = n * reach + k - 1
        ok = jnp.logical_and(tile >= 0, tile < nw)

        @pl.when(ok)
        def _(k=k):
            total = None
            for m in range(nn):
                pltpu.make_async_copy(pool.at[pl.ds(0, tall)], prcv.at[k, m], precv.at[k, m]).wait()
                goal = (lowl // xs) * cx + m * xs + lowl % xs
                keep = jnp.logical_and(goal == wide_, lowl < 2 * xs)
                term = dot(prcv[k, m], jnp.where(keep, 1.0, 0.0).astype(BF16))
                total = term if total is None else total + term
            both = total.astype(BF16)
            for j in range(2):
                spread(xp3, both[:, j * cx:(j + 1) * cx], 2 * k + j, high)

        @pl.when(jnp.logical_not(ok))
        def _(k=k):
            for dx in range(3):
                xp3[pl.ds(dx * high, tall), pl.ds(2 * k * cx, 2 * cx)] = jnp.zeros(
                    (tall, 2 * cx), BF16)

    mids = (cz + 2) * cc
    zrow = lax.broadcasted_iota(jnp.int32, (mids, 1), 0) // cc + (w * cz - 1)
    zok = jnp.logical_and(zrow >= 0, zrow < nw * cz)
    for h in range((cy + 2) // 2):
        both = conv(wc, xc3, 2 * h * cx, 2 * cx) + conv(wq, xp3, 2 * h * cx, 2 * cx)
        both = jnp.maximum(both + bc1[...], 0.0)
        ypos = lanes((mids, 2 * cx)) // cx + (n * cy - 1 + 2 * h)
        yok = jnp.logical_and(ypos >= 0, ypos < nn * cy)
        both = jnp.where(jnp.logical_and(zok, yok), both, 0.0).astype(BF16)
        for j in range(2):
            spread(x3m, both[:, j * cx:(j + 1) * cx], 2 * h + j, mids)
    for h in range(cy // 2):
        both = jnp.maximum(conv(wm, x3m, 2 * h * cx, 2 * cx) + bc2[...], 0.0).astype(BF16)
        near = dot(wp[...], both).astype(BF16)
        for j in range(2):
            cout[2 * h + j] = both[:, j * cx:(j + 1) * cx]
            ctx[2 * h + j] = near[:, j * cx:(j + 1) * cx]

    slab = cz * cf

    def context_copy(k, m):
        return remote(ctx.at[pl.ds(2 * k, 2)],
                      crcv.at[:, pl.ds(pl.multiple_of(w * slab, slab), slab)],
                      tsend.at[k, m], trecv.at[w], n * reach + k, m)

    def context_step(start):
        def step(i, carry):
            k, m = i // nn, i % nn
            self_ = jnp.logical_and(n * reach + k == w, m == n)

            @pl.when(jnp.logical_not(self_))
            def _():
                copy = context_copy(k, m)
                if start:
                    copy.start()
                else:
                    copy.wait_send()

            if start:
                @pl.when(self_)
                def _():
                    pltpu.make_async_copy(
                        ctx.at[pl.ds(2 * k, 2)],
                        crcv.at[:, pl.ds(pl.multiple_of(w * slab, slab), slab)],
                        trecv.at[w]).start()

            return carry

        lax.fori_loop(0, reach * nn, step, 0)

    context_step(True)
    bands(k2)
    receive(second)
    expand(lambda y: hidden[y], halo2, side2)
    for a in range(nw):
        pltpu.make_async_copy(ctx.at[pl.ds(0, 2)], crcv.at[:, pl.ds(a * slab, slab)],
                              trecv.at[a]).wait()
    grow = jnp.where(source == target // 4 + n * xs, 1.0, 0.0).astype(BF16)
    for g in range(fy // 4):
        more = dot(crcv[g], grow) + b2[...]
        for h in range(2):
            y = g * 4 + h * 2
            both = conv(band, x3, y * cx, 2 * cx)
            for k in range(2):
                out[y + k] = (both[:, k * cx:(k + 1) * cx] + more).astype(BF16)

    sent(first)
    sent(cmade)
    sent(second)
    each_target(False)
    context_step(False)


def local(fine_in, coarse_in, w1, b1, w2, b2, wc1, bc1, wc2, bc2, w_proj):
    nw, nn = lax.axis_size("wide"), lax.axis_size("narrow")
    cf, depth, fy, fx = fine_in.shape
    cc, cz, cy, cx = coarse_in.shape
    xs = fx // 4
    rows, crow, reach = depth * cf, cz * cc, cy // 2
    fine = fine_in.transpose(2, 1, 0, 3).reshape(fy, rows, fx)
    coarse = coarse_in.transpose(2, 1, 0, 3).reshape(cy, crow, cx)

    def base(kernel):
        o, i = kernel.shape[:2]
        return kernel.transpose(3, 4, 0, 2, 1).reshape(9, o, 3 * i).astype(F32)

    def fine_base(kernel):
        flat = base(kernel)
        gap = jnp.zeros((9, cf, rows - 3 * cf), F32)
        return jnp.concatenate([flat[:, :, cf:], gap, flat[:, :, :cf]], axis=2)

    def widened(kernel, width):
        flat = base(kernel)
        return jnp.pad(flat, ((0, 0), (0, 0), (0, width - flat.shape[2])))

    high = -(-(cz + 4) * cf // 128) * 128
    mids = (cz + 2) * cc
    tall = (cz + 4) * cf
    args = (
        fine, coarse, fine_base(w1), fine_base(w2),
        widened(wc1[:, :cc], (cz + 4) * cc), widened(wc1[:, cc:], high), widened(wc2, mids),
        jnp.tile(b1, depth)[:, None], jnp.tile(b2, depth)[:, None],
        jnp.tile(bc1, cz + 2)[:, None], jnp.tile(bc2, cz)[:, None],
        jnp.einsum("fc,pq->pfqc", w_proj, jnp.eye(cz, dtype=BF16)).reshape(cz * cf, crow),
    )
    dims = (nw, nn, depth, cf, cc, fy, cz, cy, cx, xs)
    dma = pltpu.SemaphoreType.DMA
    vmem = pltpu.VMEM
    out, cout = pl.pallas_call(
        functools.partial(kernel, dims),
        name="unet",
        out_shape=(
            jax.ShapeDtypeStruct((fy, rows, fx), BF16),
            jax.ShapeDtypeStruct((cy, crow, cx), BF16),
        ),
        in_specs=[pl.BlockSpec(memory_space=pltpu.VMEM)] * len(args),
        out_specs=(pl.BlockSpec(memory_space=pltpu.VMEM),) * 2,
        scratch_shapes=[
            vmem((2, rows, cx), BF16), vmem((rows, cx), BF16), vmem((6, rows, cx), BF16),
            vmem((2, rows, cx), BF16), vmem((rows, cx), BF16), vmem((6, rows, cx), BF16),
            vmem((3, rows, 3 * rows), BF16), vmem((3 * rows, (fy + 2) * cx), BF16),
            vmem((fy, rows, cx), BF16),
            vmem((cy + 4, 3 * crow, cx), BF16), vmem((rows + 4 * cf, cx), BF16),
            vmem((reach + 2, nn, tall, cx), BF16),
            vmem((3 * 3 * crow, (cy + 4) * cx), BF16), vmem((3 * high, (cy + 4) * cx), BF16),
            vmem((3, mids, 9 * crow), BF16), vmem((3, mids, 3 * high), BF16),
            vmem((3 * mids, (cy + 2) * cx), BF16), vmem((3, crow, 3 * mids), BF16),
            vmem((cy, cz * cf, cx), BF16), vmem((2, rows, cx), BF16),
            dma((8,)), dma((8,)), dma((8,)), dma((8,)), dma((8,)), dma((8,)),
            dma((3, nw)), dma((reach + 2, nn)), dma((reach, nn)), dma((nw,)), dma,
        ],
        compiler_params=pltpu.CompilerParams(
            collective_id=0, has_side_effects=True, vmem_limit_bytes=63 << 20),
    )(*args)
    fine_out = out.reshape(fy, depth, cf, fx).transpose(2, 1, 0, 3)
    coarse_out = cout.reshape(cy, cz, cc, cx).transpose(2, 1, 0, 3)
    return fine_out, coarse_out


def solution(mesh):
    return jax.shard_map(
        local,
        mesh=mesh,
        in_specs=(
            P(None, None, "wide", "narrow"),
            P(None, "wide", "narrow", None),
        ) + (P(),) * 9,
        out_specs=(P(None, None, "wide", "narrow"), P(None, "wide", "narrow", None)),
        check_vma=False,
    )
```

time: 274 us -> 70.3 us (0.26)
  the two profiles are of different devices: /device:TPU:1 before, /device:TPU:19 now
where the time goes in v1:
time: 70.3 us; the launch traced here: 69.9 us
  Pallas kernels  49.3 us (70%)
  local copies, waits for them, and re-layouts  16.2 us (23%)
  other arithmetic  3.58 us (5%)
  between operations  0.77 us (1%)
    pallas_call x1, Pallas kernels, local(): pl.pallas_call(functools.partial(kernel, dims), name='unet', out_shape=(j...  49.3 us
    unnamed x25, local copies, waits for them, and re-layouts  5.62 us
    pad x3, other arithmetic, widened(): return jnp.pad(flat, ((0, 0), (0, 0), (0, width - flat.shape[2])))  2.62 us
    reshape x1, local copies, waits for them, and re-layouts, local(): fine_out = out.reshape(fy, depth, cf, fx).transpose(2, 1, 0, 3)  2.21 us
    convert_element_type x10, local copies, waits for them, and re-layouts, base(): return kernel.transpose(3, 4, 0, 2, 1).reshape(9, o, 3 * i).astype(F32)  1.68 us

profile of v1, /device:TPU:19, one launch (start us, length us, event | category | flops | bytes accessed | tf_op | source)
XLA Modules:
  0.0 69.9 jit_solution(15344763410834128391)
XLA Ops:
  0.7 0.6 copy-done.11
  1.4 0.6 copy-done.8
  1.9 0.7 copy-done.9
  2.6 0.7 copy-done.10
  3.3 0.7 copy-done.7
  4.0 0.7 reshape.40.wp
  4.7 0.8 %broadcast_in_dim_tile.19.bc2 = f32[128,1]{1,0:T(8,128)} reshape(f32[2,64]{1,0:T(2,128)S(1)} %tile.11) | data formatting | bytes 1024 | tf_op jit(solution)/shard_map/broadcast_in_dim;tile | solution.py:397
  5.5 0.8 %broadcast_in_dim_tile.17.b2 = f32[256,1]{1,0:T(8,128)} reshape(f32[16,16]{1,0:T(8,128)S(1)} %tile.9) | data formatting | bytes 2048 | tf_op jit(solution)/shard_map/broadcast_in_dim;tile | solution.py:396
  6.2 0.8 %broadcast_in_dim_tile.16.b1 = f32[256,1]{1,0:T(8,128)} reshape(f32[16,16]{1,0:T(8,128)S(1)} %tile.8) | data formatting | bytes 2048 | tf_op jit(solution)/shard_map/broadcast_in_dim;tile | solution.py:396
  7.0 0.8 %broadcast_in_dim_tile.18.bc1 = f32[256,1]{1,0:T(8,128)} reshape(f32[4,64]{1,0:T(4,128)S(1)} %tile.10) | data formatting | bytes 2048 | tf_op jit(solution)/shard_map/broadcast_in_dim;tile | solution.py:397
  7.8 0.7 copy.24
  9.1 0.8 %copy-done.6 = bf16[16,16,3,3,3]{1,0,4,3,2:T(8,128)(2,1)S(1)} copy-done((bf16[16,16,3,3,3]{1,0,4,3,2:T(8,128)(2,1)S(1)}, bf16[16,16,3,3,3]{1,0,4,3,2:T(8,128)(2,1)}, u32[]{:S(2)}) %copy-start.6) | copy-done | bytes 13848
  10.3 0.8 %pad_maximum_fusion.1 = (f32[9,16,256]{2,1,0:T(8,128)}, f32[9,16,256]{2,1,0:T(8,128)}) fusion(f32[9,16,16]{2,1,0:T(8,128)S(1)} %bitcast.32, f32[9,16,32]{2,1,0:T(8,128)S(1)} %slice.26, f32[256]{0:T(256)S(1)} %pad.28.clone, f32[9,16,16]{2,1,0:T(8,128)S(1)} %bitcast.31, f32[9,16,32]{2,1,0:T(8,128)S(1)} %slice.24), kind=kLoop, calls=%fused_computation.7 | loop fusion | flops 147456 | bytes 351232 | tf_op jit(solution)/shard_map/concatenate | solution.py:384
  11.2 0.2 copy.31
  11.7 0.9 %pad_convert_fusion.1.km = f32[9,64,256]{2,1,0:T(8,128)} fusion(bf16[9,64,192]{2,1,0:T(8,128)(2,1)S(1)} %copy.32), kind=kLoop, calls=%fused_computation.3 | loop fusion | flops 147456 | bytes 811008 | tf_op jit(solution)/shard_map/jit(_pad)/pad | solution.py:388
  12.6 0.3 copy-done
  13.4 0.7 %pad_convert_fusion.2.kp = f32[9,64,128]{2,1,0:T(8,128)} fusion(bf16[9,64,48]{2,1,0:T(8,128)(2,1)S(1)} %copy.30), kind=kLoop, calls=%fused_computation.8 | loop fusion | flops 73728 | bytes 350208 | tf_op jit(solution)/shard_map/jit(_pad)/pad | solution.py:388
  14.2 0.2 copy.27
  14.7 0.8 %copy-done.1 = bf16[16,16,8,128]{3,2,1,0:T(8,128)(2,1)S(1)} copy-done((bf16[16,16,8,128]{3,2,1,0:T(8,128)(2,1)S(1)}, bf16[16,16,8,128]{3,2,1,0:T(8,128)(2,1)}, u32[]{:S(2)}) %copy-start.1) | copy-done | bytes 524312
  15.5 1.1 %copy.23 = bf16[8,16,16,128]{3,2,1,0:T(8,128)(2,1)} copy(bf16[8,16,16,128]{3,0,1,2:T(8,128)(2,1)S(1)} %bitcast.34) | data formatting | bytes 1048576 | tf_op jit(solution)/shard_map/transpose | solution.py:374
  16.6 1.0 %pad_convert_fusion.kc = f32[9,64,384]{2,1,0:T(8,128)} fusion(bf16[9,64,192]{2,1,0:T(8,128)(2,1)S(1)} %copy.28), kind=kLoop, calls=%fused_computation.1 | loop fusion | flops 221184 | bytes 1105920 | tf_op jit(solution)/shard_map/jit(_pad)/pad | solution.py:388
  17.6 49.3 %unet.1 = (bf16[8,256,128]{2,1,0:T(8,128)(2,1)}, bf16[4,128,128]{2,1,0:T(8,128)(2,1)}) custom-call(bf16[8,256,128]{2,1,0:T(8,128)(2,1)} %bitcast.28, bf16[4,128,128]{2,1,0:T(8,128)(2,1)} %bitcast.33, f32[9,16,256]{2,1,0:T(8,128)} %get-tuple-element.7.k1, f32[9,16,256]{2,1,0:T(8,128)} %get-tuple-element.6.k2, f32[9,64,384]{2,1,0:T(8,128)} %pad_convert_fusion.kc, ...), custom_call_target="tpu_custom_call" | custom-call | tf_op jit(solution)/shard_map/unet/pallas_call | solution.py:403
  67.0 2.2 %copy.42 = bf16[8,16,16,128]{3,0,1,2:T(8,128)(2,1)} copy(bf16[8,16,16,128]{3,2,1,0:T(8,128)(2,1)} %bitcast.35) | data formatting | bytes 1048576 | tf_op jit(solution)/shard_map/reshape | solution.py:429
  69.2 0.8 %copy.43 = bf16[4,2,64,128]{3,0,1,2:T(4,128)(2,1)} copy(bf16[4,2,64,128]{3,2,1,0:T(8,128)(2,1)S(1)} %bitcast.40) | data formatting | bytes 262144 | tf_op jit(solution)/shard_map/reshape | solution.py:430
  (38 shorter events, 2.3 us)
Async XLA Ops:
  0.6 0.7 copy-start.11
  1.3 0.7 copy-start.8
  1.9 0.7 copy-start.9
  2.6 0.7 copy-start.10
  3.3 0.7 copy-start.7
  6.2 1.5 %copy-start.3 = (bf16[64,2,4,128]{3,2,1,0:T(4,128)(2,1)S(1)}, bf16[64,2,4,128]{3,2,1,0:T(4,128)(2,1)}, u32[]{:S(2)}) copy-start(bf16[64,2,4,128]{3,2,1,0:T(4,128)(2,1)} %param.12) | copy-start | bytes 393220
  7.8 0.9 %copy-start.5 = (bf16[16,16,3,3,3]{1,0,4,3,2:T(8,128)(2,1)S(1)}, bf16[16,16,3,3,3]{1,0,4,3,2:T(8,128)(2,1)}, u32[]{:S(2)}) copy-start(bf16[16,16,3,3,3]{1,0,4,3,2:T(8,128)(2,1)} %param.13) | copy-start | bytes 41476
  9.0 0.9 %copy-start.6 = (bf16[16,16,3,3,3]{1,0,4,3,2:T(8,128)(2,1)S(1)}, bf16[16,16,3,3,3]{1,0,4,3,2:T(8,128)(2,1)}, u32[]{:S(2)}) copy-start(bf16[16,16,3,3,3]{1,0,4,3,2:T(8,128)(2,1)} %param.15) | copy-start | bytes 41476
  10.2 1.0 %copy-start.2 = (bf16[64,64,3,3,3]{1,0,4,3,2:T(8,128)(2,1)S(1)}, bf16[64,64,3,3,3]{1,0,4,3,2:T(8,128)(2,1)}, u32[]{:S(2)}) copy-start(bf16[64,64,3,3,3]{1,0,4,3,2:T(8,128)(2,1)} %param.19) | copy-start | bytes 663556
  11.7 1.2 %copy-start = (bf16[64,80,3,3,3]{1,0,4,3,2:T(8,128)(2,1)S(1)}, bf16[64,80,3,3,3]{1,0,4,3,2:T(8,128)(2,1)}, u32[]{:S(2)}) copy-start(bf16[64,80,3,3,3]{1,0,4,3,2:T(8,128)(2,1)} %param.17) | copy-start | bytes 829444
  14.4 1.0 %copy-start.1 = (bf16[16,16,8,128]{3,2,1,0:T(8,128)(2,1)S(1)}, bf16[16,16,8,128]{3,2,1,0:T(8,128)(2,1)}, u32[]{:S(2)}) copy-start(bf16[16,16,8,128]{3,2,1,0:T(8,128)(2,1)} %param.11) | copy-start | bytes 1572868
  66.9 2.2 %copy-start.4 = (bf16[4,128,128]{2,1,0:T(8,128)(2,1)S(1)}, bf16[4,128,128]{2,1,0:T(8,128)(2,1)}, u32[]{:S(2)}) copy-start(bf16[4,128,128]{2,1,0:T(8,128)(2,1)} %get-tuple-element.5) | copy-start | bytes 393220

commit v2 on v1

--- a/solution.py
+++ b/solution.py
@@ -20,7 +20,7 @@
 
 def kernel(
     dims,
-    fine, coarse, k1, k2, kc, kp, km, b1, b2, bc1, bc2, wp,
+    fine, coarse, k1, k2, k3, k4, b1_, b2_, bc1_, bc2_, wp,
     out, cout,
     halo1, edge1, side1, halo2, edge2, side2, band, x3, hidden,
     cbuf, pool, prcv, xc3, xp3, wc, wq, x3m, wm, ctx, crcv,
@@ -59,14 +59,32 @@
 
     lane = lanes((rows, cx))
 
+    def column(bias, copies):
+        size = bias.shape[1]
+        square = jnp.broadcast_to(bias[...], (size, size))
+        diagonal = lax.broadcasted_iota(jnp.int32, (size, size), 0) == lanes((size, size))
+        one = jnp.sum(jnp.where(diagonal, square, 0.0), axis=1, keepdims=True)
+        return jnp.concatenate([one] * copies, axis=0)
+
+    b1, b2 = column(b1_, depth), column(b2_, depth)
+    bc1, bc2 = column(bc1_, cz + 2), column(bc2_, cz)
+
+    def taps(weights, tap, start, size, width, wrap):
+        parts = [weights[dz * 9 + tap][:, start:start + size].astype(F32) for dz in range(3)]
+        gap = jnp.zeros((parts[0].shape[0], width - 3 * size), F32)
+        if wrap:
+            return jnp.concatenate([parts[1], parts[2], gap, parts[0]], axis=1)
+        return jnp.concatenate(parts + [gap], axis=1)
+
     def pack(row_of, edge):
         total = jnp.zeros((rows, cx), F32)
         for y in range(fy):
             row = row_of(y).astype(F32)
             first = pltpu.roll(row, y, 1) if y else row
             total = jnp.where(lane == y, first, total)
-            total = jnp.where(lane == 64 + y, pltpu.roll(row, 65 + y, 1), total)
-        edge[...] = total.astype(BF16)
+            last = pltpu.roll(row, fy + 1 + y, 1)
+            total = jnp.where(lane == fy + y, last, total)
+        edge[...] = total.T[:2 * fy].astype(BF16)
 
     around = ((-1, 0), (1, 0), (0, -1), (0, 1), (-1, -1), (-1, 1), (1, -1), (1, 1))
 
@@ -102,7 +120,9 @@
             pl.when(inside(a, b))(copy.wait_send)
 
     def expand(row_of, halo, side):
-        left, right, ul, ur, dl, dr = [side[i].astype(F32) for i in range(6)]
+        gap = jnp.zeros((cx - 2 * fy, rows), F32)
+        left, right, ul, ur, dl, dr = [
+            jnp.concatenate([side[i].astype(F32), gap], axis=0).T for i in range(6)]
         for y in range(-1, fy + 1):
             if y < 0:
                 raw, lcol, rcol, j = halo[0], ul, ur, fy - 1
@@ -114,7 +134,7 @@
             cols = pl.ds((y + 1) * cx, cx)
             x3[pl.ds(rows, rows), cols] = raw
             x3[pl.ds(0, rows), cols] = jnp.where(
-                lane == 0, pltpu.roll(lcol, 64 - j, 1), pltpu.roll(row, 1, 1)).astype(BF16)
+                lane == 0, pltpu.roll(lcol, cx - fy - j, 1), pltpu.roll(row, 1, 1)).astype(BF16)
             moved = pltpu.roll(rcol, cx - 1 - j, 1)
             x3[pl.ds(2 * rows, rows), cols] = jnp.where(
                 lane == cx - 1, moved, pltpu.roll(row, cx - 1, 1)).astype(BF16)
@@ -123,7 +143,7 @@
         spot = lanes((cf, rows))
         for tap in range(9):
             dy, dx = tap // 3, tap % 3
-            piece = base[tap]
+            piece = taps(base, tap, 0, cf, rows, True)
             for z in range(depth):
                 part = pltpu.roll(piece, z * cf, 1) if z else piece
                 if z == 0:
@@ -132,11 +152,11 @@
                     part = jnp.where(spot < cf, 0.0, part)
                 band[dy, pl.ds(z * cf, cf), pl.ds(dx * rows, rows)] = part.astype(BF16)
 
-    def short_bands(base, target, count, step):
-        size, width = base.shape[1], base.shape[2]
+    def short_bands(base, target, count, start, step):
+        size, width = base.shape[1], target.shape[2] // 3
         for tap in range(9):
             dy, dx = tap // 3, tap % 3
-            piece = base[tap]
+            piece = taps(base, tap, start, step, width, False)
             for z in range(count):
                 part = pltpu.roll(piece, z * step, 1) if z else piece
                 target[dy, pl.ds(z * size, size), pl.ds(dx * width, width)] = part.astype(BF16)
@@ -163,14 +183,14 @@
                       remote(src, dst, csend.at[i], crecv.at[i], w - da, n - db)))
     pl.semaphore_wait(barrier, nw * nn - 1)
     send(first)
-    send(cmade)
     clear(first)
     clear(cmade)
     cbuf[pl.ds(2, cy), pl.ds(crow, crow), :] = coarse[...]
-    pool[pl.ds(0, 2 * cf), :] = jnp.zeros((2 * cf, cx), BF16)
-    pool[pl.ds(2 * cf + rows, 2 * cf), :] = jnp.zeros((2 * cf, cx), BF16)
+    pool[pl.ds(0, cf), :] = jnp.zeros((cf, cx), BF16)
+    pool[pl.ds(cf + rows // 2, cf), :] = jnp.zeros((cf, cx), BF16)
     bands(k1)
     receive(first)
+    send(cmade)
     expand(lambda y: fine[y], halo1, side1)
 
     source = lax.broadcasted_iota(jnp.int32, (cx, cx), 0)
@@ -180,7 +200,7 @@
         total = None
         for h in range(2):
             y = g * 4 + h * 2
-            both = jnp.maximum(conv(band, x3, y * cx, 2 * cx) + b1[...], 0.0).astype(BF16)
+            both = jnp.maximum(conv(band, x3, y * cx, 2 * cx) + b1, 0.0).astype(BF16)
             for k in range(2):
                 row = both[:, k * cx:(k + 1) * cx]
                 hidden[y + k] = row
@@ -190,18 +210,25 @@
             summed = total
         else:
             summed = summed + total
-    pool[pl.ds(2 * cf, rows), :] = (summed * (1.0 / 16.0)).astype(BF16)
+    mean = summed * (1.0 / 16.0)
+    turned = pltpu.roll(mean, cx // 2, 1)
+    for z in range(depth // 2):
+        first_z = mean[2 * z * cf:(2 * z + 1) * cf]
+        pool[pl.ds((z + 1) * cf, cf), :] = (
+            first_z + turned[(2 * z + 1) * cf:(2 * z + 2) * cf]).astype(BF16)
 
     tall = (cz + 4) * cf
+    half = tall // 2
+    step_z = cz // 2 * cf
 
     def pooled_copy(a, which, b):
         k = w - b * reach + 1
-        return remote(pool.at[pl.ds(pl.multiple_of(a * cz * cf, cf), tall)], prcv.at[k, n],
+        return remote(pool.at[pl.ds(pl.multiple_of(a * step_z, cf), half)], prcv.at[k, n],
                       psend.at[which, a], precv.at[k, n], a, b)
 
     def local_copy():
         k = w - n * reach + 1
-        return pltpu.make_async_copy(pool.at[pl.ds(pl.multiple_of(w * cz * cf, cf), tall)],
+        return pltpu.make_async_copy(pool.at[pl.ds(pl.multiple_of(w * step_z, cf), half)],
                                      prcv.at[k, n], precv.at[k, n])
 
     home = w // reach
@@ -245,9 +272,9 @@
     send(second)
     clear(second)
 
-    short_bands(kc, wc, cz + 2, cc)
-    short_bands(kp, wq, cz + 2, cf)
-    short_bands(km, wm, cz, cc)
+    short_bands(k3, wc, cz + 2, 0, cc)
+    short_bands(k3, wq, cz + 2, cc, cf)
+    short_bands(k4, wm, cz, 0, cc)
     receive(cmade)
 
     def spread(field, raw, y, height):
@@ -267,8 +294,12 @@
         for dx in range(3):
             xp3[pl.ds(dx * high + tall, high - tall), :] = jnp.zeros(
                 (high - tall, xp3.shape[1]), BF16)
-    lowl = lax.broadcasted_iota(jnp.int32, (cx, 2 * cx), 0)
-    wide_ = lanes((cx, 2 * cx))
+    lowl = lax.broadcasted_iota(jnp.int32, (cx, 4 * cx), 0)
+    wide_ = lanes((cx, 4 * cx))
+    settle = []
+    for m in range(nn):
+        goal = lowl // xs * cx + m * xs + lowl % xs
+        settle.append(jnp.where(goal == wide_, 1.0, 0.0).astype(BF16))
     for k in range(reach + 2):
         tile = n * reach + k - 1
         ok = jnp.logical_and(tile >= 0, tile < nw)
@@ -277,14 +308,16 @@
         def _(k=k):
             total = None
             for m in range(nn):
-                pltpu.make_async_copy(pool.at[pl.ds(0, tall)], prcv.at[k, m], precv.at[k, m]).wait()
-                goal = (lowl // xs) * cx + m * xs + lowl % xs
-                keep = jnp.logical_and(goal == wide_, lowl < 2 * xs)
-                term = dot(prcv[k, m], jnp.where(keep, 1.0, 0.0).astype(BF16))
+                pltpu.make_async_copy(pool.at[pl.ds(0, half)], prcv.at[k, m], precv.at[k, m]).wait()
+                term = dot(prcv[k, m], settle[m])
                 total = term if total is None else total + term
-            both = total.astype(BF16)
             for j in range(2):
-                spread(xp3, both[:, j * cx:(j + 1) * cx], 2 * k + j, high)
+                even = total[:, j * cx:(j + 1) * cx]
+                odd = total[:, (2 + j) * cx:(3 + j) * cx]
+                parts = []
+                for z in range(half // cf):
+                    parts += [even[z * cf:(z + 1) * cf], odd[z * cf:(z + 1) * cf]]
+                spread(xp3, jnp.concatenate(parts, axis=0).astype(BF16), 2 * k + j, high)
 
         @pl.when(jnp.logical_not(ok))
         def _(k=k):
@@ -297,25 +330,29 @@
     zok = jnp.logical_and(zrow >= 0, zrow < nw * cz)
     for h in range((cy + 2) // 2):
         both = conv(wc, xc3, 2 * h * cx, 2 * cx) + conv(wq, xp3, 2 * h * cx, 2 * cx)
-        both = jnp.maximum(both + bc1[...], 0.0)
+        both = jnp.maximum(both + bc1, 0.0)
         ypos = lanes((mids, 2 * cx)) // cx + (n * cy - 1 + 2 * h)
         yok = jnp.logical_and(ypos >= 0, ypos < nn * cy)
         both = jnp.where(jnp.logical_and(zok, yok), both, 0.0).astype(BF16)
         for j in range(2):
             spread(x3m, both[:, j * cx:(j + 1) * cx], 2 * h + j, mids)
     for h in range(cy // 2):
-        both = jnp.maximum(conv(wm, x3m, 2 * h * cx, 2 * cx) + bc2[...], 0.0).astype(BF16)
-        near = dot(wp[...], both).astype(BF16)
+        both = jnp.maximum(conv(wm, x3m, 2 * h * cx, 2 * cx) + bc2, 0.0).astype(BF16)
+        near = jnp.concatenate(
+            [dot(wp[...], both[z * cc:(z + 1) * cc]) for z in range(cz)], axis=0)
+        group = lanes((cf, cx)) // xs
+        for m in range(nn):
+            total = jnp.zeros((cf, cx), F32)
+            for j in range(2):
+                for z in range(cz):
+                    piece = near[z * cf:(z + 1) * cf, j * cx:(j + 1) * cx]
+                    spot = j * cz + z
+                    turn = (spot - m) * xs % cx
+                    piece = pltpu.roll(piece, turn, 1) if turn else piece
+                    total = jnp.where(group == spot, piece, total)
+            ctx[h, m] = total.astype(BF16)
         for j in range(2):
             cout[2 * h + j] = both[:, j * cx:(j + 1) * cx]
-            ctx[2 * h + j] = near[:, j * cx:(j + 1) * cx]
-
-    slab = cz * cf
-
-    def context_copy(k, m):
-        return remote(ctx.at[pl.ds(2 * k, 2)],
-                      crcv.at[:, pl.ds(pl.multiple_of(w * slab, slab), slab)],
-                      tsend.at[k, m], trecv.at[w], n * reach + k, m)
 
     def context_step(start):
         def step(i, carry):
@@ -324,7 +361,8 @@
 
             @pl.when(jnp.logical_not(self_))
             def _():
-                copy = context_copy(k, m)
+                copy = remote(ctx.at[k, m], crcv.at[w], tsend.at[k, m], trecv.at[w],
+                              n * reach + k, m)
                 if start:
                     copy.start()
                 else:
@@ -333,10 +371,7 @@
             if start:
                 @pl.when(self_)
                 def _():
-                    pltpu.make_async_copy(
-                        ctx.at[pl.ds(2 * k, 2)],
-                        crcv.at[:, pl.ds(pl.multiple_of(w * slab, slab), slab)],
-                        trecv.at[w]).start()
+                    pltpu.make_async_copy(ctx.at[k, m], crcv.at[w], trecv.at[w]).start()
 
             return carry
 
@@ -347,11 +382,17 @@
     receive(second)
     expand(lambda y: hidden[y], halo2, side2)
     for a in range(nw):
-        pltpu.make_async_copy(ctx.at[pl.ds(0, 2)], crcv.at[:, pl.ds(a * slab, slab)],
-                              trecv.at[a]).wait()
-    grow = jnp.where(source == target // 4 + n * xs, 1.0, 0.0).astype(BF16)
+        pltpu.make_async_copy(ctx.at[0, 0], crcv.at[a], trecv.at[a]).wait()
+    near = jnp.concatenate([crcv[a] for a in range(nw)], axis=0)
     for g in range(fy // 4):
-        more = dot(crcv[g], grow) + b2[...]
+        grown = []
+        for z in range(cz):
+            grow = jnp.where(source == target // 4 + (g * cz + z) * xs, 1.0, 0.0)
+            grown.append(dot(near, grow.astype(BF16)))
+        parts = []
+        for a in range(nw):
+            parts += [one[a * cf:(a + 1) * cf] for one in grown]
+        more = jnp.concatenate(parts, axis=0) + b2
         for h in range(2):
             y = g * 4 + h * 2
             both = conv(band, x3, y * cx, 2 * cx)
@@ -374,28 +415,16 @@
     fine = fine_in.transpose(2, 1, 0, 3).reshape(fy, rows, fx)
     coarse = coarse_in.transpose(2, 1, 0, 3).reshape(cy, crow, cx)
 
-    def base(kernel):
+    def flat(kernel):
         o, i = kernel.shape[:2]
-        return kernel.transpose(3, 4, 0, 2, 1).reshape(9, o, 3 * i).astype(F32)
-
-    def fine_base(kernel):
-        flat = base(kernel)
-        gap = jnp.zeros((9, cf, rows - 3 * cf), F32)
-        return jnp.concatenate([flat[:, :, cf:], gap, flat[:, :, :cf]], axis=2)
-
-    def widened(kernel, width):
-        flat = base(kernel)
-        return jnp.pad(flat, ((0, 0), (0, 0), (0, width - flat.shape[2])))
+        return kernel.transpose(2, 3, 4, 0, 1).reshape(27, o, i)
 
     high = -(-(cz + 4) * cf // 128) * 128
     mids = (cz + 2) * cc
     tall = (cz + 4) * cf
     args = (
-        fine, coarse, fine_base(w1), fine_base(w2),
-        widened(wc1[:, :cc], (cz + 4) * cc), widened(wc1[:, cc:], high), widened(wc2, mids),
-        jnp.tile(b1, depth)[:, None], jnp.tile(b2, depth)[:, None],
-        jnp.tile(bc1, cz + 2)[:, None], jnp.tile(bc2, cz)[:, None],
-        jnp.einsum("fc,pq->pfqc", w_proj, jnp.eye(cz, dtype=BF16)).reshape(cz * cf, crow),
+        fine, coarse, flat(w1), flat(w2), flat(wc1), flat(wc2),
+        b1[None], b2[None], bc1[None], bc2[None], w_proj,
     )
     dims = (nw, nn, depth, cf, cc, fy, cz, cy, cx, xs)
     dma = pltpu.SemaphoreType.DMA
@@ -410,16 +439,16 @@
         in_specs=[pl.BlockSpec(memory_space=pltpu.VMEM)] * len(args),
         out_specs=(pl.BlockSpec(memory_space=pltpu.VMEM),) * 2,
         scratch_shapes=[
-            vmem((2, rows, cx), BF16), vmem((rows, cx), BF16), vmem((6, rows, cx), BF16),
-            vmem((2, rows, cx), BF16), vmem((rows, cx), BF16), vmem((6, rows, cx), BF16),
+            vmem((2, rows, cx), BF16), vmem((2 * fy, rows), BF16), vmem((6, 2 * fy, rows), BF16),
+            vmem((2, rows, cx), BF16), vmem((2 * fy, rows), BF16), vmem((6, 2 * fy, rows), BF16),
             vmem((3, rows, 3 * rows), BF16), vmem((3 * rows, (fy + 2) * cx), BF16),
             vmem((fy, rows, cx), BF16),
-            vmem((cy + 4, 3 * crow, cx), BF16), vmem((rows + 4 * cf, cx), BF16),
-            vmem((reach + 2, nn, tall, cx), BF16),
+            vmem((cy + 4, 3 * crow, cx), BF16), vmem((rows // 2 + 2 * cf, cx), BF16),
+            vmem((reach + 2, nn, tall // 2, cx), BF16),
             vmem((3 * 3 * crow, (cy + 4) * cx), BF16), vmem((3 * high, (cy + 4) * cx), BF16),
             vmem((3, mids, 9 * crow), BF16), vmem((3, mids, 3 * high), BF16),
             vmem((3 * mids, (cy + 2) * cx), BF16), vmem((3, crow, 3 * mids), BF16),
-            vmem((cy, cz * cf, cx), BF16), vmem((2, rows, cx), BF16),
+            vmem((reach, nn, cf, cx), BF16), vmem((nw, cf, cx), BF16),
             dma((8,)), dma((8,)), dma((8,)), dma((8,)), dma((8,)), dma((8,)),
             dma((3, nw)), dma((reach + 2, nn)), dma((reach, nn)), dma((nw,)), dma,
         ],

time: 70.3 us -> 49 us (0.70)
  the two profiles are of different devices: /device:TPU:19 before, /device:TPU:1 now
where the time goes in v2:
time: 49 us; the launch traced here: 48.3 us
  Pallas kernels  41 us (84%)
  local copies, waits for them, and re-layouts  6.73 us (14%)
  between operations  0.65 us (1%)
    pallas_call x1, Pallas kernels, local(): pl.pallas_call(functools.partial(kernel, dims), name='unet', out_shape=(j...  41 us
    reshape x1, local copies, waits for them, and re-layouts, local(): fine_out = out.reshape(fy, depth, cf, fx).transpose(2, 1, 0, 3)  2.21 us
    transpose x1, local copies, waits for them, and re-layouts, local(): fine = fine_in.transpose(2, 1, 0, 3).reshape(fy, rows, fx)  2.18 us
    transpose x1, local copies, waits for them, and re-layouts, local(): coarse = coarse_in.transpose(2, 1, 0, 3).reshape(cy, crow, cx)  1.58 us

profile of v2, /device:TPU:1, one launch (start us, length us, event | category | flops | bytes accessed | tf_op | source)
XLA Modules:
  0.0 48.3 jit_solution(11188954871223925539)
XLA Ops:
  0.6 1.6 %copy.14 = bf16[4,2,64,128]{3,2,1,0:T(8,128)(2,1)} copy(bf16[4,2,64,128]{3,0,1,2:T(4,128)(2,1)} %bitcast.35) | data formatting | bytes 262144 | tf_op jit(solution)/shard_map/transpose | solution.py:416
  2.2 2.2 %copy.13 = bf16[8,16,16,128]{3,2,1,0:T(8,128)(2,1)} copy(bf16[8,16,16,128]{3,0,1,2:T(8,128)(2,1)} %bitcast.29) | data formatting | bytes 1048576 | tf_op jit(solution)/shard_map/transpose | solution.py:415
  4.4 41.0 %unet.1 = (bf16[8,256,128]{2,1,0:T(8,128)(2,1)}, bf16[4,128,128]{2,1,0:T(8,128)(2,1)}) custom-call(bf16[8,256,128]{2,1,0:T(8,128)(2,1)} %bitcast.28, bf16[4,128,128]{2,1,0:T(8,128)(2,1)} %bitcast.32, bf16[27,16,16]{2,1,0:T(8,128)(2,1)} %bitcast.38, bf16[27,16,16]{2,1,0:T(8,128)(2,1)} %bitcast.39, bf16[27,64,80]{2,1,0:T(8,128)(2,1)} %bitcast.33, ...), custom_call_target="tpu_custom_call" | custom-call | tf_op jit(solution)/shard_map/unet/pallas_call | solution.py:432
  45.4 0.0 copy-start
  45.4 2.2 %copy.19 = bf16[8,16,16,128]{3,0,1,2:T(8,128)(2,1)} copy(bf16[8,16,16,128]{3,2,1,0:T(8,128)(2,1)} %bitcast.31) | data formatting | bytes 1048576 | tf_op jit(solution)/shard_map/reshape | solution.py:458
  47.6 0.0 copy-done
  47.6 0.8 %copy.20 = bf16[4,2,64,128]{3,0,1,2:T(4,128)(2,1)} copy(bf16[4,2,64,128]{3,2,1,0:T(8,128)(2,1)S(1)} %bitcast.37) | data formatting | bytes 262144 | tf_op jit(solution)/shard_map/reshape | solution.py:459
Async XLA Ops:
  45.4 2.2 %copy-start = (bf16[4,128,128]{2,1,0:T(8,128)(2,1)S(1)}, bf16[4,128,128]{2,1,0:T(8,128)(2,1)}, u32[]{:S(2)}) copy-start(bf16[4,128,128]{2,1,0:T(8,128)(2,1)} %get-tuple-element.5) | copy-start | bytes 393220

commit v3 on v2

--- a/solution.py
+++ b/solution.py
@@ -20,8 +20,9 @@
 
 def kernel(
     dims,
-    fine, coarse, k1, k2, k3, k4, b1_, b2_, bc1_, bc2_, wp,
+    fine_in, coarse_in, k1, k2, k3, k4, b1_, b2_, bc1_, bc2_, wp,
     out, cout,
+    fine, coarse, partial, held,
     halo1, edge1, side1, halo2, edge2, side2, band, x3, hidden,
     cbuf, pool, prcv, xc3, xp3, wc, wq, x3m, wm, ctx, crcv,
     fsend, frecv, hsend, hrecv, csend, crecv, psend, precv, tsend, trecv, lsem,
@@ -58,6 +59,11 @@
         return jnp.logical_and(ok_a, ok_b)
 
     lane = lanes((rows, cx))
+    for z in range(depth):
+        fine[:, pl.ds(z * cf, cf), :] = jnp.swapaxes(fine_in[:, z].astype(F32), 0, 1).astype(BF16)
+    for z in range(cz):
+        coarse[:, pl.ds(z * cc, cc), :] = jnp.swapaxes(
+            coarse_in[:, z].astype(F32), 0, 1).astype(BF16)
 
     def column(bias, copies):
         size = bias.shape[1]
@@ -189,6 +195,9 @@
     pool[pl.ds(0, cf), :] = jnp.zeros((cf, cx), BF16)
     pool[pl.ds(cf + rows // 2, cf), :] = jnp.zeros((cf, cx), BF16)
     bands(k1)
+    short_bands(k3, wc, cz + 2, 0, cc)
+    short_bands(k3, wq, cz + 2, cc, cf)
+    short_bands(k4, wm, cz, 0, cc)
     receive(first)
     send(cmade)
     expand(lambda y: fine[y], halo1, side1)
@@ -272,9 +281,6 @@
     send(second)
     clear(second)
 
-    short_bands(k3, wc, cz + 2, 0, cc)
-    short_bands(k3, wq, cz + 2, cc, cf)
-    short_bands(k4, wm, cz, 0, cc)
     receive(cmade)
 
     def spread(field, raw, y, height):
@@ -294,6 +300,8 @@
         for dx in range(3):
             xp3[pl.ds(dx * high + tall, high - tall), :] = jnp.zeros(
                 (high - tall, xp3.shape[1]), BF16)
+    for h in range((cy + 2) // 2):
+        partial[h] = conv(wc, xc3, 2 * h * cx, 2 * cx)
     lowl = lax.broadcasted_iota(jnp.int32, (cx, 4 * cx), 0)
     wide_ = lanes((cx, 4 * cx))
     settle = []
@@ -329,7 +337,7 @@
     zrow = lax.broadcasted_iota(jnp.int32, (mids, 1), 0) // cc + (w * cz - 1)
     zok = jnp.logical_and(zrow >= 0, zrow < nw * cz)
     for h in range((cy + 2) // 2):
-        both = conv(wc, xc3, 2 * h * cx, 2 * cx) + conv(wq, xp3, 2 * h * cx, 2 * cx)
+        both = partial[h] + conv(wq, xp3, 2 * h * cx, 2 * cx)
         both = jnp.maximum(both + bc1, 0.0)
         ypos = lanes((mids, 2 * cx)) // cx + (n * cy - 1 + 2 * h)
         yok = jnp.logical_and(ypos >= 0, ypos < nn * cy)
@@ -381,6 +389,8 @@
     bands(k2)
     receive(second)
     expand(lambda y: hidden[y], halo2, side2)
+    for h in range(fy // 2):
+        held[h] = conv(band, x3, 2 * h * cx, 2 * cx)
     for a in range(nw):
         pltpu.make_async_copy(ctx.at[0, 0], crcv.at[a], trecv.at[a]).wait()
     near = jnp.concatenate([crcv[a] for a in range(nw)], axis=0)
@@ -395,7 +405,7 @@
         more = jnp.concatenate(parts, axis=0) + b2
         for h in range(2):
             y = g * 4 + h * 2
-            both = conv(band, x3, y * cx, 2 * cx)
+            both = held[y // 2]
             for k in range(2):
                 out[y + k] = (both[:, k * cx:(k + 1) * cx] + more).astype(BF16)
 
@@ -412,8 +422,6 @@
     cc, cz, cy, cx = coarse_in.shape
     xs = fx // 4
     rows, crow, reach = depth * cf, cz * cc, cy // 2
-    fine = fine_in.transpose(2, 1, 0, 3).reshape(fy, rows, fx)
-    coarse = coarse_in.transpose(2, 1, 0, 3).reshape(cy, crow, cx)
 
     def flat(kernel):
         o, i = kernel.shape[:2]
@@ -423,7 +431,7 @@
     mids = (cz + 2) * cc
     tall = (cz + 4) * cf
     args = (
-        fine, coarse, flat(w1), flat(w2), flat(wc1), flat(wc2),
+        fine_in, coarse_in, flat(w1), flat(w2), flat(wc1), flat(wc2),
         b1[None], b2[None], bc1[None], bc2[None], w_proj,
     )
     dims = (nw, nn, depth, cf, cc, fy, cz, cy, cx, xs)
@@ -439,6 +447,8 @@
         in_specs=[pl.BlockSpec(memory_space=pltpu.VMEM)] * len(args),
         out_specs=(pl.BlockSpec(memory_space=pltpu.VMEM),) * 2,
         scratch_shapes=[
+            vmem((fy, rows, cx), BF16), vmem((cy, crow, cx), BF16),
+            vmem(((cy + 2) // 2, mids, 2 * cx), F32), vmem((fy // 2, rows, 2 * cx), F32),
             vmem((2, rows, cx), BF16), vmem((2 * fy, rows), BF16), vmem((6, 2 * fy, rows), BF16),
             vmem((2, rows, cx), BF16), vmem((2 * fy, rows), BF16), vmem((6, 2 * fy, rows), BF16),
             vmem((3, rows, 3 * rows), BF16), vmem((3 * rows, (fy + 2) * cx), BF16),

time: 49 us -> 42.8 us (0.87)
  local copies, waits for them, and re-layouts: 6.73 us -> 2.97 us
  Pallas kernels: 41 us -> 38.6 us
    transpose x2 -> x0, local copies, waits for them, and re-layouts: 3.75 us -> none  [the longest x1 2.18 us: local(): fine = fine_in.transpose(2, 1, 0, 3).reshape(fy, rows, fx)]
    pallas_call x1, Pallas kernels: 41 us -> 38.6 us  [local(): pl.pallas_call(functools.partial(kernel, dims), name='unet', out_shape=(j...]
where the time goes in v3:
time: 42.8 us; the launch traced here: 42.2 us
  Pallas kernels  38.6 us (90%)
  local copies, waits for them, and re-layouts  2.97 us (7%)
  between operations  0.65 us (2%)
    pallas_call x1, Pallas kernels, local(): pl.pallas_call(functools.partial(kernel, dims), name='unet', out_shape=(j...  38.6 us
    reshape x1, local copies, waits for them, and re-layouts, local(): fine_out = out.reshape(fy, depth, cf, fx).transpose(2, 1, 0, 3)  2.21 us

profile of v3, /device:TPU:1, one launch (start us, length us, event | category | flops | bytes accessed | tf_op | source)
XLA Modules:
  0.0 42.2 jit_solution(1717813962683663381)
XLA Ops:
  0.6 38.6 %unet.1 = (bf16[8,256,128]{2,1,0:T(8,128)(2,1)}, bf16[4,128,128]{2,1,0:T(8,128)(2,1)}) custom-call(bf16[16,16,8,128]{3,2,1,0:T(8,128)(2,1)} %fine_in.1, bf16[64,2,4,128]{3,2,1,0:T(4,128)(2,1)} %coarse_in.1, bf16[27,16,16]{2,1,0:T(8,128)(2,1)} %bitcast.30, bf16[27,16,16]{2,1,0:T(8,128)(2,1)} %bitcast.31, bf16[27,64,80]{2,1,0:T(8,128)(2,1)} %bitcast.26, ...), custom_call_target="tpu_custom_call" | custom-call | tf_op jit(solution)/shard_map/unet/pallas_call | solution.py:440
  39.2 0.0 copy-start
  39.3 2.2 %copy.17 = bf16[8,16,16,128]{3,0,1,2:T(8,128)(2,1)} copy(bf16[8,16,16,128]{3,2,1,0:T(8,128)(2,1)} %bitcast.25) | data formatting | bytes 1048576 | tf_op jit(solution)/shard_map/reshape | solution.py:468
  41.5 0.0 copy-done
  41.5 0.8 %copy.18 = bf16[4,2,64,128]{3,0,1,2:T(4,128)(2,1)} copy(bf16[4,2,64,128]{3,2,1,0:T(8,128)(2,1)S(1)} %bitcast.29) | data formatting | bytes 262144 | tf_op jit(solution)/shard_map/reshape | solution.py:469
Async XLA Ops:
  39.2 2.2 %copy-start = (bf16[4,128,128]{2,1,0:T(8,128)(2,1)S(1)}, bf16[4,128,128]{2,1,0:T(8,128)(2,1)}, u32[]{:S(2)}) copy-start(bf16[4,128,128]{2,1,0:T(8,128)(2,1)} %get-tuple-element.5) | copy-start | bytes 393220

commit v4 on v3

--- a/solution.py
+++ b/solution.py
@@ -195,11 +195,11 @@
     pool[pl.ds(0, cf), :] = jnp.zeros((cf, cx), BF16)
     pool[pl.ds(cf + rows // 2, cf), :] = jnp.zeros((cf, cx), BF16)
     bands(k1)
+    send(cmade)
     short_bands(k3, wc, cz + 2, 0, cc)
     short_bands(k3, wq, cz + 2, cc, cf)
     short_bands(k4, wm, cz, 0, cc)
     receive(first)
-    send(cmade)
     expand(lambda y: fine[y], halo1, side1)
 
     source = lax.broadcasted_iota(jnp.int32, (cx, cx), 0)

time: 42.8 us -> 39.8 us (0.930)
  Pallas kernels: 38.6 us -> 35.6 us
    pallas_call x1, Pallas kernels: 38.6 us -> 35.6 us  [local(): pl.pallas_call(functools.partial(kernel, dims), name='unet', out_shape=(j...]
where the time goes in v4:
time: 39.8 us; the launch traced here: 39.3 us
  Pallas kernels  35.6 us (89%)
  local copies, waits for them, and re-layouts  2.97 us (7%)
  between operations  0.65 us (2%)
    pallas_call x1, Pallas kernels, local(): pl.pallas_call(functools.partial(kernel, dims), name='unet', out_shape=(j...  35.6 us
    reshape x1, local copies, waits for them, and re-layouts, local(): fine_out = out.reshape(fy, depth, cf, fx).transpose(2, 1, 0, 3)  2.21 us

profile of v4, /device:TPU:1, one launch (start us, length us, event | category | flops | bytes accessed | tf_op | source)
XLA Modules:
  0.0 39.3 jit_solution(10538972443881071752)
XLA Ops:
  0.6 35.6 %unet.1 = (bf16[8,256,128]{2,1,0:T(8,128)(2,1)}, bf16[4,128,128]{2,1,0:T(8,128)(2,1)}) custom-call(bf16[16,16,8,128]{3,2,1,0:T(8,128)(2,1)} %fine_in.1, bf16[64,2,4,128]{3,2,1,0:T(4,128)(2,1)} %coarse_in.1, bf16[27,16,16]{2,1,0:T(8,128)(2,1)} %bitcast.30, bf16[27,16,16]{2,1,0:T(8,128)(2,1)} %bitcast.31, bf16[27,64,80]{2,1,0:T(8,128)(2,1)} %bitcast.26, ...), custom_call_target="tpu_custom_call" | custom-call | tf_op jit(solution)/shard_map/unet/pallas_call | solution.py:440
  36.3 0.0 copy-start
  36.3 2.2 %copy.17 = bf16[8,16,16,128]{3,0,1,2:T(8,128)(2,1)} copy(bf16[8,16,16,128]{3,2,1,0:T(8,128)(2,1)} %bitcast.25) | data formatting | bytes 1048576 | tf_op jit(solution)/shard_map/reshape | solution.py:468
  38.5 0.0 copy-done
  38.5 0.8 %copy.18 = bf16[4,2,64,128]{3,0,1,2:T(4,128)(2,1)} copy(bf16[4,2,64,128]{3,2,1,0:T(8,128)(2,1)S(1)} %bitcast.29) | data formatting | bytes 262144 | tf_op jit(solution)/shard_map/reshape | solution.py:469
Async XLA Ops:
  36.3 2.2 %copy-start = (bf16[4,128,128]{2,1,0:T(8,128)(2,1)S(1)}, bf16[4,128,128]{2,1,0:T(8,128)(2,1)}, u32[]{:S(2)}) copy-start(bf16[4,128,128]{2,1,0:T(8,128)(2,1)} %get-tuple-element.5) | copy-start | bytes 393220
